TPU v7x, 32 devices: a whole 2x2x4 slice. The times are simulated.
32 devices in a mesh: row: 4 (over y, core), col: 4 (over z), lag: 2 (over x).
Axes of the slice: x: 2, y: 2, z: 4, core: 2. Of those that a mesh axis runs over, the one named last changes fastest.
Arguments:
- trajectories: bfloat16 [4096, 4096], P(('row', 'col'), 'lag'), may hold values from -6 to 6
- pair_live: int32 [4, 4], replicated, may hold values from 0 to 1, as said below
Outputs:
- gram: bfloat16 [4096, 4096], P(('row', 'lag'), 'col')
Inputs may be any that keep to these rules, and one draw needn't show every extreme that they name: `pair_live`: Symmetric, with every diagonal entry 1.
All inputs are finite; a program needn't handle non-finite values.
Results may differ from a plain program's by a relative error of at most 0.0015.
Values may be sent and summed in bfloat16 or wider, within the bound.
A program may use at most 64 MiB of HBM per device.

v0:
```python
import jax
import jax.numpy as jnp
from jax import lax
from jax.sharding import PartitionSpec as P


def from_root(value, axis, source):
    kept = jnp.where(lax.axis_index(axis) == source, value, 0).astype(value.dtype)
    return lax.psum(kept, axis)


def pair_distance(left, right, left_norm, right_norm):
    inner = lax.dot_general(
        left, right, (((1,), (1,)), ((), ())), preferred_element_type=jnp.float32
    )
    return left_norm[:, None] + right_norm[None, :] - 2.0 * inner


def squares(block):
    return jnp.sum(jnp.square(block.astype(jnp.float32)), axis=1)


def on_device(trajectories, pair_live):
    row_block = lax.all_gather(trajectories, "col", axis=0, tiled=True)
    col_block = from_root(row_block, "row", lax.axis_index("col"))
    live = pair_live[lax.axis_index("row"), lax.axis_index("col")]
    samples = trajectories.shape[1] * lax.axis_size("lag")
    row_norm = squares(row_block)
    col_norm = squares(col_block)
    dist = lax.psum_scatter(
        pair_distance(row_block, col_block, row_norm, col_norm),
        "lag",
        scatter_dimension=0,
        tiled=True,
    )
    gram = jnp.exp(-2.0 * dist / samples) * live.astype(jnp.float32)
    return gram.astype(jnp.bfloat16)


def solution(mesh):
    return jax.shard_map(
        on_device,
        mesh=mesh,
        in_specs=(P(("row", "col"), "lag"), P()),
        out_specs=P(("row", "lag"), "col"),
        check_vma=False,
    )
```

profile of v0, /device:TPU:24, one launch (start us, length us, event | category | flops | bytes accessed | tf_op | source)
XLA Modules:
  0.0 255.4 jit_solution(15009054547006258623)
XLA Ops:
  6.5 0.0 all-gather.2.cloned.1.call-start
  6.5 0.7 all-gather.2.cloned.1.call-update
  7.3 0.0 all-reduce.2.cloned.1.call-start
  7.3 80.6 %all-gather.2.cloned.1.call-done = bf16[1024,2048]{1,0:T(8,128)(2,1)} async-done(((bf16[256,2048]{1,0:T(8,128)(2,1)}), bf16[1024,2048]{1,0:T(8,128)(2,1)}) %all-gather.2.cloned.1.call-update) | async-done | bytes 4194320 | tf_op jit(solution)/shard_map/all_gather | solution.py:24
  87.9 2.3 broadcast_select_fusion
  90.2 0.0 all-reduce.2.cloned.1.call-update
  90.2 0.0 reduce-scatter.2.cloned.1.call-start
  90.2 3.1 %multiply_reduce_fusion.1 = f32[1024]{0:T(1024)S(1)} fusion(bf16[1024,2048]{1,0:T(8,128)(2,1)} %all-gather.2.cloned.1.call-done), kind=kLoop, calls=%fused_computation.1 | loop fusion | flops 6290432 | bytes 4198400 | tf_op jit(solution)/shard_map/reduce_sum | solution.py:20
  93.3 85.9 %all-reduce.2.cloned.1.call-done = bf16[1024,2048]{1,0:T(8,128)(2,1)} async-done(((bf16[1024,2048]{1,0:T(8,128)(2,1)}), bf16[1024,2048]{1,0:T(8,128)(2,1)}) %all-reduce.2.cloned.1.call-update) | async-done | bytes 4194320 | tf_op jit(solution)/shard_map/psum | solution.py:9
  179.2 0.0 copy-start
  179.2 3.2 %multiply_reduce_fusion = f32[1024]{0:T(1024)S(1)} fusion(bf16[1024,2048]{1,0:T(8,128)(2,1)} %all-reduce.2.cloned.1.call-done), kind=kLoop, calls=%fused_computation | loop fusion | flops 6290432 | bytes 4198400 | tf_op jit(solution)/shard_map/reduce_sum | solution.py:20
  182.5 0.2 copy-done
  182.7 8.3 %bitcast_subtract_fusion = f32[1024,1024]{0,1:T(8,128)} fusion(bf16[1024,2048]{1,0:T(8,128)(2,1)} %all-reduce.2.cloned.1.call-done, bf16[1024,2048]{1,0:T(8,128)(2,1)S(1)} %copy-done, f32[1024]{0:T(1024)S(1)} %multiply_reduce_fusion, f32[1024]{0:T(1024)S(1)} %multiply_reduce_fusion.1), kind=kOutput, calls=%fused_computation.2 | convolution fusion | flops 4298113024 | bytes 12591104 | tf_op jit(solution)/shard_map/dot_general | solution.py:13
  191.0 0.0 reduce-scatter.2.cloned.1.call-update
  191.0 1.3 dynamic_slice.3
  192.9 52.7 %reduce-scatter.2.cloned.1.call-done = f32[512,1024]{0,1:T(8,128)} async-done(((f32[1024,1024]{0,1:T(8,128)}), f32[512,1024]{0,1:T(8,128)}) %reduce-scatter.2.cloned.1.call-update) | async-done | bytes 2097168 | tf_op jit(solution)/shard_map/reduce_scatter | solution.py:30
  245.7 1.9 multiply_convert_fusion
  247.6 1.3 copy.3
Async XLA Ops:
  6.5 81.4 %all-gather.2.cloned.1.call-start = ((), (), s32[]{:S(2)}) async-start(), calls=%async_computation.1 | async-start | bytes 5242880 | tf_op jit(solution)/shard_map/all_gather | solution.py:24
  7.3 172.0 %all-reduce.2.cloned.1.call-start = ((), (), s32[]{:S(2)}) async-start(), calls=%async_computation.2 | async-start | bytes 8388608 | tf_op jit(solution)/shard_map/psum | solution.py:9
  90.2 155.5 %reduce-scatter.2.cloned.1.call-start = ((), (), s32[]{:S(2)}) async-start(), calls=%async_computation.3 | async-start | bytes 6291456 | tf_op jit(solution)/shard_map/reduce_scatter | solution.py:30
  179.2 3.4 %copy-start = (bf16[1024,2048]{1,0:T(8,128)(2,1)S(1)}, bf16[1024,2048]{1,0:T(8,128)(2,1)}, u32[]{:S(2)}) copy-start(bf16[1024,2048]{1,0:T(8,128)(2,1)} %all-gather.2.cloned.1.call-done) | copy-start | bytes 12582916
Sparse Core Ops, SparseCore 0:
  8.9 78.9 all-gather.1
  90.3 88.8 all-reduce.1
  191.1 54.5 reduce-scatter.1
where the time goes:
time: 257 us; the launch traced here: 255 us
  waiting for transfers between devices  220 us (86%)
  between operations  13.8 us (5%)
  other arithmetic  10.5 us (4%)
  matrix products  8.28 us (3%)
  local copies, waits for them, and re-layouts  2.81 us (1%)
    psum x1, waiting for transfers between devices, from_root(): return lax.psum(kept, axis)  85.9 us
    all_gather x1, waiting for transfers between devices, on_device(): row_block = lax.all_gather(trajectories, 'col', axis=0, tiled=True)  80.6 us
    reduce_scatter x1, waiting for transfers between devices, on_device(): lax.psum_scatter(pair_distance(row_block, col_block, row_norm, col_norm),...  52.7 us
    dot_general x1, matrix products, pair_distance(): lax.dot_general(left, right, (((1,), (1,)), ((), ())), preferred_element_...  8.28 us
    reduce_sum x2, other arithmetic, squares(): return jnp.sum(jnp.square(block.astype(jnp.float32)), axis=1)  6.29 us
  transfers between devices with their start and end apart: 3, of which 3 were waited for; matrix products, arithmetic and copies ran while one was open for 2% of the time, Pallas kernels for 0%

commit v1 on v0

v1 whole, which is shorter than its diff:
```python
import functools

import jax
import jax.numpy as jnp
from jax import lax
from jax.experimental import pallas as pl
from jax.experimental.pallas import tpu as pltpu
from jax.sharding import PartitionSpec as P

MESH = pl.DeviceIdType.MESH
SPLIT = 2
NT_DIMS = (((1,), (1,)), ((), ()))


def kernel(
    rows, cols, lags, split, samples,
    x_ref, live_ref, out_ref,
    rb, cb, rn, cn, tile, got,
    own_sem, z_send, z_recv, c_send, c_recv, c_copy, t_send, t_recv,
):
    r, c, l = lax.axis_index("row"), lax.axis_index("col"), lax.axis_index("lag")
    units = cols * split
    m = rb.shape[1]
    mine = units // lags
    bits = rows.bit_length() - 1
    node = lax.bitwise_xor(r, c)

    own = pltpu.make_async_copy(
        x_ref, rb.at[pl.ds(c * split, split)], own_sem
    )
    own.start()

    barrier = pltpu.get_barrier_semaphore()
    for j in range(1, rows):
        pl.semaphore_signal(
            barrier, device_id={"row": lax.rem(r + j, rows)}, device_id_type=MESH
        )
    for j in range(1, lags):
        pl.semaphore_signal(
            barrier, device_id={"lag": lax.rem(l + j, lags)}, device_id_type=MESH
        )

    @pl.when(c > 0)
    def _():
        pl.semaphore_signal(barrier, device_id={"col": c - 1}, device_id_type=MESH)

    @pl.when(c < cols - 1)
    def _():
        pl.semaphore_signal(barrier, device_id={"col": c + 1}, device_id_type=MESH)

    beside = jnp.where(jnp.logical_or(c == 0, c == cols - 1), 1, 2)
    pl.semaphore_wait(barrier, rows - 1 + lags - 1 + beside)
    own.wait()

    def along(side, u):
        to = jnp.clip(c + 1 - 2 * side, 0, cols - 1)
        return pltpu.make_async_remote_copy(
            rb.at[u], rb.at[u], z_send.at[side, u], z_recv.at[u],
            device_id={"col": to}, device_id_type=MESH,
        )

    def down(bit, src, u):
        return pltpu.make_async_remote_copy(
            src.at[u], cb.at[u], c_send.at[bit, u], c_recv.at[u],
            device_id={"row": lax.bitwise_xor(r, 1 << bit)}, device_id_type=MESH,
        )

    def local(u):
        return pltpu.make_async_copy(rb.at[u], cb.at[u], c_copy.at[u])

    def has_child(bit):
        return lax.rem(node, 2 << bit) == 0

    def across(i, j):
        owner = i // mine
        hop = lax.rem(owner - l + lags, lags)
        slot = jnp.maximum(hop - 1, 0)
        return pltpu.make_async_remote_copy(
            tile.at[i, j], got.at[slot, lax.rem(i, mine), j],
            t_send.at[i, j], t_recv.at[slot, lax.rem(i, mine), j],
            device_id={"lag": owner}, device_id_type=MESH,
        )

    def valid(side, d):
        k = c - d if side == 0 else c + d
        return jnp.logical_and(k >= 0, k < cols), k

    def goes_on(side):
        return c < cols - 1 if side == 0 else c > 0

    def rank(u):
        return jnp.abs(u // split - c) * split + lax.rem(u, split)

    def one_round(q, carry):
        d, s = q // split, lax.rem(q, split)
        for side in range(2):
            ok, k = valid(side, d)
            u = jnp.clip(k, 0, cols - 1) * split + s

            @pl.when(jnp.logical_and(ok, d > 0))
            def _():
                along(side, u).wait_recv()

            @pl.when(jnp.logical_and(ok, goes_on(side)))
            def _():
                along(side, u).start()

            first = jnp.logical_and(ok, jnp.logical_or(d > 0, side == 0))

            @pl.when(jnp.logical_and(first, node == 0))
            def _():
                for bit in reversed(range(bits)):
                    down(bit, rb, u).start()
                local(u).start()

        for side in range(2):
            ok, k = valid(side, d)
            u = jnp.clip(k, 0, cols - 1) * split + s
            first = jnp.logical_and(ok, jnp.logical_or(d > 0, side == 0))

            @pl.when(first)
            def _():
                a = rb[u].astype(jnp.float32)
                rn[u] = jnp.broadcast_to(
                    jnp.sum(a * a, axis=1, keepdims=True), rn.shape[1:]
                )

            @pl.when(jnp.logical_and(first, node == 0))
            def _():
                local(u).wait()

            @pl.when(jnp.logical_and(first, node != 0))
            def _():
                down(0, cb, u).wait_recv()
                for bit in reversed(range(bits)):

                    @pl.when(has_child(bit))
                    def _():
                        down(bit, cb, u).start()

            @pl.when(first)
            def _():
                b = cb[u].astype(jnp.float32)
                n = jnp.broadcast_to(jnp.sum(b * b, axis=1, keepdims=True), (m, 128))
                cn[u] = n.T[:8]

        def one_tile(p, carry):
            i0, j = p // units, lax.rem(p, units)
            i = lax.rem(i0 + (l + 1) * mine, units)

            @pl.when(jnp.maximum(rank(i), rank(j)) == q)
            def _():
                inner = lax.dot_general(
                    rb[i], cb[j], NT_DIMS, preferred_element_type=jnp.float32
                )
                tile[i, j] = rn[i][:, :1] + cn[j][:1] - 2.0 * inner

                @pl.when(i // mine != l)
                def _():
                    across(i, j).start()

            return carry

        return lax.fori_loop(0, units * units, one_tile, carry)

    lax.fori_loop(0, units, one_round, 0)

    live = live_ref[r, c].astype(jnp.float32)

    def finish(kk, carry):
        i = l * mine + kk
        for j in range(units):
            total = tile[i, j]
            for o in range(lags - 1):
                pltpu.make_async_remote_copy(
                    tile.at[i, j], got.at[o, kk, j], t_send.at[i, j],
                    t_recv.at[o, kk, j],
                    device_id={"lag": lax.rem(l + 1, lags)}, device_id_type=MESH,
                ).wait_recv()
                total = total + got[o, kk, j]
            gram = jnp.exp(-2.0 * total / samples) * live
            out_ref[pl.ds(kk * m, m), j * m : (j + 1) * m] = gram.astype(out_ref.dtype)
        return carry

    lax.fori_loop(0, mine, finish, 0)

    def drain(u, carry):
        k = u // split

        @pl.when(jnp.logical_and(k <= c, c < cols - 1))
        def _():
            along(0, u).wait_send()

        @pl.when(jnp.logical_and(k >= c, c > 0))
        def _():
            along(1, u).wait_send()

        for bit in range(bits):

            @pl.when(has_child(bit))
            def _():
                down(bit, cb, u).wait_send()

        @pl.when(u // mine != l)
        def _():
            def each(j, carry):
                across(u, j).wait_send()
                return carry

            lax.fori_loop(0, units, each, 0)

        return carry

    lax.fori_loop(0, units, drain, 0)


def on_device(rows, cols, lags, trajectories, pair_live):
    held, width = trajectories.shape
    split = SPLIT if held % (SPLIT * 128) == 0 else 1
    m = held // split
    units = cols * split
    mine = units // lags
    bits = rows.bit_length() - 1
    dma = pltpu.SemaphoreType.DMA
    return pl.pallas_call(
        functools.partial(kernel, rows, cols, lags, split, width * lags),
        out_shape=jax.ShapeDtypeStruct((mine * m, units * m), jnp.bfloat16),
        in_specs=[
            pl.BlockSpec(memory_space=pl.ANY),
            pl.BlockSpec(memory_space=pltpu.SMEM),
        ],
        out_specs=pl.BlockSpec(memory_space=pltpu.VMEM),
        scratch_shapes=[
            pltpu.VMEM((units, m, width), jnp.bfloat16),
            pltpu.VMEM((units, m, width), jnp.bfloat16),
            pltpu.VMEM((units, m, 128), jnp.float32),
            pltpu.VMEM((units, 8, m), jnp.float32),
            pltpu.VMEM((units, units, m, m), jnp.float32),
            pltpu.VMEM((lags - 1, mine, units, m, m), jnp.float32),
            dma,
            dma((2, units)),
            dma((units,)),
            dma((bits, units)),
            dma((units,)),
            dma((units,)),
            dma((units, units)),
            dma((lags - 1, mine, units)),
        ],
        compiler_params=pltpu.CompilerParams(
            collective_id=0, has_side_effects=True, vmem_limit_bytes=60 * 2**20
        ),
    )(trajectories.reshape(split, m, width), pair_live)


def solution(mesh):
    size = mesh.shape
    return jax.shard_map(
        functools.partial(on_device, size["row"], size["col"], size["lag"]),
        mesh=mesh,
        in_specs=(P(("row", "col"), "lag"), P()),
        out_specs=P(("row", "lag"), "col"),
        check_vma=False,
    )
```

time: 257 us -> 105 us (0.41)
  the two profiles are of different devices: /device:TPU:24 before, /device:TPU:7 now
where the time goes in v1:
time: 105 us
  Pallas kernels  103 us (98%)
  local copies, waits for them, and re-layouts  2.26 us (2%)
    pallas_call x1, Pallas kernels, on_device(): pl.pallas_call(functools.partial(kernel, rows, cols, lags, split, width *...  103 us
    unnamed x1, local copies, waits for them, and re-layouts  2.26 us

profile of v1, /device:TPU:7, one launch (start us, length us, event | category | flops | bytes accessed | tf_op | source)
XLA Modules:
  0.0 105.2 jit_solution(14789289109916304482)
XLA Ops:
  0.0 102.9 %shard_map.28 = bf16[512,1024]{1,0:T(8,128)(2,1)} custom-call(bf16[2,128,2048]{2,1,0:T(8,128)(2,1)} %bitcast.1, s32[4,4]{1,0:T(4,128)} %live_ref.1), custom_call_target="tpu_custom_call" | custom-call | tf_op jit(solution)/shard_map/pallas_call | solution.py:225
  102.9 2.3 %copy.4 = bf16[512,1024]{1,0:T(8,128)(2,1)} copy(bf16[512,1024]{1,0:T(8,128)(2,1)} %shard_map.28) | data formatting | bytes 2097152

commit v2 on v1

--- a/solution.py
+++ b/solution.py
@@ -88,11 +88,39 @@
     def goes_on(side):
         return c < cols - 1 if side == 0 else c > 0
 
-    def rank(u):
-        return jnp.abs(u // split - c) * split + lax.rem(u, split)
+    half = cols // lags
+    final = (cols - 1) * split - 1
+
+    def is_late(where, lag):
+        if split == 1 or cols < 3:
+            return False
+        return jnp.logical_or(
+            jnp.logical_and(where == 0, 1 // half == lag),
+            jnp.logical_and(where == cols - 1, (cols - 2) // half == lag),
+        )
+
+    def arrival(q):
+        p = q - split
+        moved = jnp.where(p == final, split - 1, jnp.where(p >= split - 1, p + 1, p))
+        return jnp.where(is_late(c, l), split + moved, q)
+
+    def rank(u, lag):
+        q = jnp.abs(u // split - c) * split + lax.rem(u, split)
+        n = q - split
+        moved = jnp.where(n == split - 1, final, jnp.where(n > split - 1, n - 1, n))
+        return jnp.where(
+            jnp.logical_and(is_late(c, lag), n >= 0), split + moved, q
+        )
+
+    def holds_back(side):
+        if split == 1 or cols < 3:
+            return False
+        to = c + 1 - 2 * side
+        return jnp.logical_and(to == (cols - 1 if side == 0 else 0), is_late(to, l))
 
     def one_round(q, carry):
-        d, s = q // split, lax.rem(q, split)
+        e = jnp.where(q >= split, arrival(q), q)
+        d, s = e // split, lax.rem(e, split)
         for side in range(2):
             ok, k = valid(side, d)
             u = jnp.clip(k, 0, cols - 1) * split + s
@@ -101,9 +129,19 @@
             def _():
                 along(side, u).wait_recv()
 
-            @pl.when(jnp.logical_and(ok, goes_on(side)))
+            held_back = jnp.logical_and(holds_back(side), q == split - 1)
+
+            @pl.when(
+                jnp.logical_and(
+                    jnp.logical_and(ok, goes_on(side)), jnp.logical_not(held_back)
+                )
+            )
             def _():
                 along(side, u).start()
+
+            @pl.when(jnp.logical_and(holds_back(side), q == final))
+            def _():
+                along(side, c * split + split - 1).start()
 
             first = jnp.logical_and(ok, jnp.logical_or(d > 0, side == 0))
 
@@ -148,7 +186,7 @@
             i0, j = p // units, lax.rem(p, units)
             i = lax.rem(i0 + (l + 1) * mine, units)
 
-            @pl.when(jnp.maximum(rank(i), rank(j)) == q)
+            @pl.when(jnp.maximum(rank(i, l), rank(j, l)) == q)
             def _():
                 inner = lax.dot_general(
                     rb[i], cb[j], NT_DIMS, preferred_element_type=jnp.float32
@@ -167,22 +205,35 @@
 
     live = live_ref[r, c].astype(jnp.float32)
 
-    def finish(kk, carry):
+    def finish(last, kk, carry):
         i = l * mine + kk
         for j in range(units):
-            total = tile[i, j]
-            for o in range(lags - 1):
-                pltpu.make_async_remote_copy(
-                    tile.at[i, j], got.at[o, kk, j], t_send.at[i, j],
-                    t_recv.at[o, kk, j],
-                    device_id={"lag": lax.rem(l + 1, lags)}, device_id_type=MESH,
-                ).wait_recv()
-                total = total + got[o, kk, j]
-            gram = jnp.exp(-2.0 * total / samples) * live
-            out_ref[pl.ds(kk * m, m), j * m : (j + 1) * m] = gram.astype(out_ref.dtype)
+            comes_last = False
+            for o in range(1, lags):
+                sender = lax.rem(l + o, lags)
+                at = jnp.maximum(rank(i, sender), rank(j, sender))
+                comes_last = jnp.logical_or(comes_last, at == units - 1)
+
+            @pl.when(comes_last == last)
+            def _():
+                total = tile[i, j]
+                for o in range(lags - 1):
+                    pltpu.make_async_remote_copy(
+                        tile.at[i, j], got.at[o, kk, j], t_send.at[i, j],
+                        t_recv.at[o, kk, j],
+                        device_id={"lag": lax.rem(l + 1, lags)},
+                        device_id_type=MESH,
+                    ).wait_recv()
+                    total = total + got[o, kk, j]
+                gram = jnp.exp(-2.0 * total / samples) * live
+                out_ref[pl.ds(kk * m, m), j * m : (j + 1) * m] = gram.astype(
+                    out_ref.dtype
+                )
+
         return carry
 
-    lax.fori_loop(0, mine, finish, 0)
+    for last in (False, True):
+        lax.fori_loop(0, mine, functools.partial(finish, last), 0)
 
     def drain(u, carry):
         k = u // split

time: 105 us -> 104 us (level)
  the two profiles are of different devices: /device:TPU:7 before, /device:TPU:24 now
where the time goes in v2:
time: 104 us
  Pallas kernels  101 us (97%)
  local copies, waits for them, and re-layouts  2.26 us (2%)
    pallas_call x1, Pallas kernels, on_device(): pl.pallas_call(functools.partial(kernel, rows, cols, lags, split, width *...  101 us
    unnamed x1, local copies, waits for them, and re-layouts  2.26 us

profile of v2, /device:TPU:24, one launch (start us, length us, event | category | flops | bytes accessed | tf_op | source)
XLA Modules:
  0.0 103.5 jit_solution(1600264768945519866)
XLA Ops:
  0.0 101.3 %shard_map.28 = bf16[512,1024]{1,0:T(8,128)(2,1)} custom-call(bf16[2,128,2048]{2,1,0:T(8,128)(2,1)} %bitcast.1, s32[4,4]{1,0:T(4,128)} %live_ref.1), custom_call_target="tpu_custom_call" | custom-call | tf_op jit(solution)/shard_map/pallas_call | solution.py:276
  101.3 2.3 %copy.4 = bf16[512,1024]{1,0:T(8,128)(2,1)} copy(bf16[512,1024]{1,0:T(8,128)(2,1)} %shard_map.28) | data formatting | bytes 2097152

commit v3 on v2

v3 whole, which is shorter than its diff:
```python
import functools

import jax
import jax.numpy as jnp
from jax import lax
from jax.experimental import pallas as pl
from jax.experimental.pallas import tpu as pltpu
from jax.sharding import PartitionSpec as P

MESH = pl.DeviceIdType.MESH
SPLIT = 2
SUB = 1
NT_DIMS = (((1,), (1,)), ((), ()))


def kernel(
    rows, cols, lags, split, samples,
    x_ref, live_ref, out_ref,
    rb, rn, cn, tile, got,
    own_sem, z_send, z_recv, c_send, c_recv, t_send, t_recv,
):
    r, c, l = lax.axis_index("row"), lax.axis_index("col"), lax.axis_index("lag")
    units = cols * split
    m = rb.shape[1]
    mine = units // lags
    bits = rows.bit_length() - 1
    node = lax.bitwise_xor(r, c)
    base = jnp.where(node == 0, 0, units)

    own = pltpu.make_async_copy(
        x_ref, rb.at[pl.ds(c * split, split)], own_sem
    )
    own.start()

    barrier = pltpu.get_barrier_semaphore()
    for j in range(1, rows):
        pl.semaphore_signal(
            barrier, device_id={"row": lax.rem(r + j, rows)}, device_id_type=MESH
        )
    for j in range(1, lags):
        pl.semaphore_signal(
            barrier, device_id={"lag": lax.rem(l + j, lags)}, device_id_type=MESH
        )

    @pl.when(c > 0)
    def _():
        pl.semaphore_signal(barrier, device_id={"col": c - 1}, device_id_type=MESH)

    @pl.when(c < cols - 1)
    def _():
        pl.semaphore_signal(barrier, device_id={"col": c + 1}, device_id_type=MESH)

    beside = jnp.where(jnp.logical_or(c == 0, c == cols - 1), 1, 2)
    pl.semaphore_wait(barrier, rows - 1 + lags - 1 + beside)
    own.wait()

    chunk = m // SUB

    def part(ref, u, h):
        return ref.at[u, pl.ds(h * chunk, chunk)]

    def along(side, u, h):
        to = jnp.clip(c + 1 - 2 * side, 0, cols - 1)
        return pltpu.make_async_remote_copy(
            part(rb, u, h), part(rb, u, h), z_send.at[side, u, h], z_recv.at[u, h],
            device_id={"col": to}, device_id_type=MESH,
        )

    def down(bit, u, h):
        return pltpu.make_async_remote_copy(
            part(rb, base + u, h), part(rb, units + u, h), c_send.at[bit, u, h], c_recv.at[u, h],
            device_id={"row": lax.bitwise_xor(r, 1 << bit)}, device_id_type=MESH,
        )

    def has_child(bit):
        return lax.rem(node, 2 << bit) == 0

    def across(i, j):
        owner = i // mine
        hop = lax.rem(owner - l + lags, lags)
        slot = jnp.maximum(hop - 1, 0)
        return pltpu.make_async_remote_copy(
            tile.at[i, j], got.at[slot, lax.rem(i, mine), j],
            t_send.at[i, j], t_recv.at[slot, lax.rem(i, mine), j],
            device_id={"lag": owner}, device_id_type=MESH,
        )

    def valid(side, d):
        k = c - d if side == 0 else c + d
        return jnp.logical_and(k >= 0, k < cols), k

    def goes_on(side):
        return c < cols - 1 if side == 0 else c > 0

    half = cols // lags
    final = (cols - 1) * split - 1

    def is_late(where, lag):
        if split == 1 or cols < 3:
            return False
        return jnp.logical_or(
            jnp.logical_and(where == 0, 1 // half == lag),
            jnp.logical_and(where == cols - 1, (cols - 2) // half == lag),
        )

    def arrival(q):
        p = q - split
        moved = jnp.where(p == final, split - 1, jnp.where(p >= split - 1, p + 1, p))
        return jnp.where(jnp.logical_and(is_late(c, l), p >= 0), split + moved, q)

    def last_unit(lag):
        far = jnp.where(2 * c < cols, cols - 1, 0)
        near = jnp.where(c == 0, 1, cols - 2)
        return jnp.where(is_late(c, lag), near, far) * split + split - 1

    def holds_back(side):
        if split == 1 or cols < 3:
            return False
        to = c + 1 - 2 * side
        return jnp.logical_and(to == (cols - 1 if side == 0 else 0), is_late(to, l))

    def unit_at(q, side):
        e = arrival(q)
        d = e // split
        ok, k = valid(side, d)
        u = jnp.clip(k, 0, cols - 1) * split + e - d * split
        return ok, jnp.logical_and(ok, jnp.logical_or(d > 0, side == 0)), u

    def one_round(q, carry):
        d = arrival(q) // split
        here = [unit_at(q, side) for side in range(2)]

        def unit(side):
            return here[side]

        def one_chunk(h, carry):
            for side in range(2):
                ok, first, u = unit(side)

                @pl.when(jnp.logical_and(ok, d > 0))
                def _():
                    along(side, u, h).wait_recv()

                held_back = jnp.logical_and(holds_back(side), q == split - 1)

                @pl.when(
                    jnp.logical_and(
                        jnp.logical_and(ok, goes_on(side)), jnp.logical_not(held_back)
                    )
                )
                def _():
                    along(side, u, h).start()

                @pl.when(jnp.logical_and(holds_back(side), q == final))
                def _():
                    along(side, c * split + split - 1, h).start()

                @pl.when(jnp.logical_and(first, node == 0))
                def _():
                    for bit in reversed(range(bits)):
                        down(bit, u, h).start()

            for side in range(2):
                ok, first, u = unit(side)

                @pl.when(jnp.logical_and(first, node != 0))
                def _():
                    down(0, u, h).wait_recv()
                    for bit in reversed(range(bits)):

                        @pl.when(has_child(bit))
                        def _():
                            down(bit, u, h).start()

            return carry

        lax.fori_loop(0, SUB, one_chunk, 0)

        for side in range(2):
            ok, first, u = unit(side)

            @pl.when(first)
            def _():
                a = rb[u].astype(jnp.float32)
                rn[u] = jnp.broadcast_to(
                    jnp.sum(a * a, axis=1, keepdims=True), rn.shape[1:]
                )
                b = rb[base + u].astype(jnp.float32)
                n = jnp.broadcast_to(jnp.sum(b * b, axis=1, keepdims=True), (m, 128))
                cn[u] = n.T[:8]

        def one_tile(i, j, leaves):
            @pl.when((i // mine != l) == leaves)
            def _():
                inner = lax.dot_general(
                    rb[i], rb[base + j], NT_DIMS, preferred_element_type=jnp.float32
                )
                tile[i, j] = rn[i][:, :1] + cn[j][:1] - 2.0 * inner
                if leaves:
                    across(i, j).start()

        def pairs(leaves, p, carry):
            q2, side2 = p // 2, lax.rem(p, 2)
            e = arrival(q2)
            d2 = e // split
            k = c + jnp.where(side2 == 0, -d2, d2)
            found = jnp.logical_and(k >= 0, k < cols)
            found = jnp.logical_and(found, jnp.logical_or(d2 > 0, side2 == 0))
            v = jnp.clip(k, 0, cols - 1) * split + e - d2 * split
            for side in range(2):
                _, first, u = unit(side)

                @pl.when(jnp.logical_and(first, found))
                def _():
                    one_tile(u, v, leaves)

                    @pl.when(q2 < q)
                    def _():
                        one_tile(v, u, leaves)

            return carry

        for leaves in (True, False):
            lax.fori_loop(0, 2 * q + 2, functools.partial(pairs, leaves), 0)
        return carry

    lax.fori_loop(0, units, one_round, 0)

    live = live_ref[r, c].astype(jnp.float32)

    def finish(last, kk, carry):
        i = l * mine + kk
        for j in range(units):
            comes_last = False
            for o in range(1, lags):
                end = last_unit(lax.rem(l + o, lags))
                comes_last = jnp.logical_or(
                    comes_last, jnp.logical_or(i == end, j == end)
                )

            @pl.when(comes_last == last)
            def _():
                total = tile[i, j]
                for o in range(lags - 1):
                    pltpu.make_async_remote_copy(
                        tile.at[i, j], got.at[o, kk, j], t_send.at[i, j],
                        t_recv.at[o, kk, j],
                        device_id={"lag": lax.rem(l + 1, lags)},
                        device_id_type=MESH,
                    ).wait_recv()
                    total = total + got[o, kk, j]
                gram = jnp.exp(-2.0 * total / samples) * live
                out_ref[pl.ds(kk * m, m), j * m : (j + 1) * m] = gram.astype(
                    out_ref.dtype
                )

        return carry

    for last in (False, True):
        lax.fori_loop(0, mine, functools.partial(finish, last), 0)

    def drain(u, carry):
        k = u // split
        for h in range(SUB):

            @pl.when(jnp.logical_and(k <= c, c < cols - 1))
            def _():
                along(0, u, h).wait_send()

            @pl.when(jnp.logical_and(k >= c, c > 0))
            def _():
                along(1, u, h).wait_send()

            for bit in range(bits):

                @pl.when(has_child(bit))
                def _():
                    down(bit, u, h).wait_send()

        @pl.when(u // mine != l)
        def _():
            def each(j, carry):
                across(u, j).wait_send()
                return carry

            lax.fori_loop(0, units, each, 0)

        return carry

    lax.fori_loop(0, units, drain, 0)


def on_device(rows, cols, lags, trajectories, pair_live):
    held, width = trajectories.shape
    split = SPLIT if held % (SPLIT * 128) == 0 else 1
    m = held // split
    units = cols * split
    mine = units // lags
    bits = rows.bit_length() - 1
    dma = pltpu.SemaphoreType.DMA
    return pl.pallas_call(
        functools.partial(kernel, rows, cols, lags, split, width * lags),
        out_shape=jax.ShapeDtypeStruct((mine * m, units * m), jnp.bfloat16),
        in_specs=[
            pl.BlockSpec(memory_space=pl.ANY),
            pl.BlockSpec(memory_space=pltpu.SMEM),
        ],
        out_specs=pl.BlockSpec(memory_space=pltpu.VMEM),
        scratch_shapes=[
            pltpu.VMEM((2 * units, m, width), jnp.bfloat16),
            pltpu.VMEM((units, m, 128), jnp.float32),
            pltpu.VMEM((units, 8, m), jnp.float32),
            pltpu.VMEM((units, units, m, m), jnp.float32),
            pltpu.VMEM((lags - 1, mine, units, m, m), jnp.float32),
            dma,
            dma((2, units, SUB)),
            dma((units, SUB)),
            dma((bits, units, SUB)),
            dma((units, SUB)),
            dma((units, units)),
            dma((lags - 1, mine, units)),
        ],
        compiler_params=pltpu.CompilerParams(
            collective_id=0, has_side_effects=True, vmem_limit_bytes=60 * 2**20
        ),
    )(trajectories.reshape(split, m, width), pair_live)


def solution(mesh):
    size = mesh.shape
    return jax.shard_map(
        functools.partial(on_device, size["row"], size["col"], size["lag"]),
        mesh=mesh,
        in_specs=(P(("row", "col"), "lag"), P()),
        out_specs=P(("row", "lag"), "col"),
        check_vma=False,
    )
```

time: 104 us -> 103 us (level)
    pallas_call x1, Pallas kernels: 101 us -> 100 us  [on_device(): pl.pallas_call(functools.partial(kernel, rows, cols, lags, split, width *...]
where the time goes in v3:
time: 103 us; the launch traced here: 102 us
  Pallas kernels  100 us (97%)
  local copies, waits for them, and re-layouts  2.26 us (2%)
    pallas_call x1, Pallas kernels, on_device(): pl.pallas_call(functools.partial(kernel, rows, cols, lags, split, width *...  100 us
    unnamed x1, local copies, waits for them, and re-layouts  2.26 us

profile of v3, /device:TPU:24, one launch (start us, length us, event | category | flops | bytes accessed | tf_op | source)
XLA Modules:
  0.0 102.4 jit_solution(1295015426390058179)
XLA Ops:
  0.0 100.2 %shard_map.28 = bf16[512,1024]{1,0:T(8,128)(2,1)} custom-call(bf16[2,128,2048]{2,1,0:T(8,128)(2,1)} %bitcast.1, s32[4,4]{1,0:T(4,128)} %live_ref.1), custom_call_target="tpu_custom_call" | custom-call | tf_op jit(solution)/shard_map/pallas_call | solution.py:301
  100.2 2.3 %copy.4 = bf16[512,1024]{1,0:T(8,128)(2,1)} copy(bf16[512,1024]{1,0:T(8,128)(2,1)} %shard_map.28) | data formatting | bytes 2097152
